TPU v7x, 256 devices: a whole 4x4x8 slice. The times are simulated.
256 devices in a mesh: slab: 64 (over z, x, core), dom: 4 (over y).
Axes of the slice: x: 4, y: 4, z: 8, core: 2. Of those that a mesh axis runs over, the one named last changes fastest.
Arguments:
- elem_grad: float32 [3, 8, 1376256], P(None, None, ('slab', 'dom')), may hold values from -3 to 3
- elem_stress: float32 [6, 1376256], P(None, ('slab', 'dom')), may hold values from -6 to 6
- elem_grade: int32 [1376256], P(('slab', 'dom')), may hold values from 0 to 15
- grade_scale: float32 [16], replicated, may hold values from 0.5 to 2
- part_counts: int32 [64, 4], P('slab'), may hold values from 1 to 5376, as said below
- node_lists: int32 [4, 128, 8, 512], P(None, 'slab', None, 'dom'), may hold values from -1 to 7167, as said below
- stiff_diag: float32 [3, 128, 8, 512], P(None, 'slab', None, 'dom'), may hold values from 1 to 4
- start_block: float32 [3, 32, 128, 8, 512], P(None, None, 'slab', None, 'dom'), may hold values from -600 to 600
Outputs:
- next_block: float32 [3, 32, 128, 8, 512], P(None, None, 'slab', None, 'dom')
- diag_blocks: float32 [2, 32, 32], replicated
- offdiag_blocks: float32 [3, 32, 32], replicated
Inputs may be any that keep to these rules, and one draw needn't show every extreme that they name: `part_counts`: each row sums to 7168, the elements of one slab; in every slab one partition holds exactly 5376. node_lists[j, f, x, y] is the pool number, within the slab of floor f, of the element of layer f whose in-plane base corner is (x - j mod 2, (y - j // 2) mod 512); it is -1 exactly where x - j mod 2 lies outside 0 to 6. Every element of a slab appears at its four in-plane corners.
All inputs are finite; a program needn't handle non-finite values.
Results may differ from a plain program's by a relative error of at most 0.0003.
Values sent between devices are 32-bit elements; how exact they have to be, the bound alone decides.
No kernel may reach another device: no remote copies, remote signals or barrier semaphores. Data moves between devices by JAX's collectives and lax.ppermute only.
A program may use at most 128 MiB of HBM per device.

v0:
```python
import jax
import jax.numpy as jnp
import numpy as np
from jax import lax
from jax.sharding import PartitionSpec as P

highest = lax.Precision.HIGHEST


def extended_2(cells, sides, width):
    for axis, dim in sides:
        count = lax.axis_size(axis)
        ends = count - 1
        head = lax.slice_in_dim(cells, 0, width, axis=dim)
        tail = lax.slice_in_dim(cells, cells.shape[dim] - width, cells.shape[dim], axis=dim)
        cells = jnp.concatenate(
            [
                lax.ppermute(tail, axis, [(i, (i + 1) % count) for i in range(ends)]),
                cells,
                lax.ppermute(head, axis, [((i + 1) % count, i) for i in range(ends)]),
            ],
            axis=dim,
        )
    return cells


def from_behind(value, axis, steps):
    count = lax.axis_size(axis)
    pairs = [(source, (source + steps) % count) for source in range(count)]
    return lax.ppermute(value, axis, pairs)


def passed_along(block, axis, distance):
    devices = range(lax.axis_size(axis))
    route = [(i - distance, i) for i in devices if i - distance in devices]
    return lax.ppermute(block, axis, route)


def offset_table(quad_slot, layer_side):
    table = np.zeros((8, 27))
    shift_x = quad_slot % 2
    shift_y = quad_slot // 2
    for corner in range(8):
        corner_x = corner % 2
        corner_y = corner // 2 % 2
        corner_z = corner // 4
        target = (
            corner_x - shift_x + 1 + 3 * (corner_y - shift_y + 1) + 9 * (corner_z - layer_side + 1)
        )
        table[corner, target] = 1.0
    return jnp.asarray(table, dtype=jnp.float32)


def stress_matrix(stress):
    return jnp.stack(
        [
            jnp.stack([stress[0], stress[5], stress[4]]),
            jnp.stack([stress[5], stress[1], stress[3]]),
            jnp.stack([stress[4], stress[3], stress[2]]),
        ]
    )


def grade_lookup(grades, table):
    levels = jnp.arange(table.shape[0], dtype=jnp.int32)[:, None]
    onehot = (grades[None, :] == levels).astype(jnp.float32)
    return jnp.dot(table, onehot, precision=highest)


def element_matrices(gradients, stress, scales):
    pushed = jnp.einsum("ik...,kb...->ib...", stress_matrix(stress), gradients, precision=highest)
    return jnp.einsum("ia...,ib...->ab...", gradients, pushed, precision=highest) * scales


def pool_columns(slot_lists, counts, capacity):
    offsets = jnp.cumsum(counts) - counts
    shaped = offsets.reshape((-1,) + (1,) * slot_lists.ndim)
    pool_ids = jnp.maximum(slot_lists, 0)
    partition = jnp.sum((pool_ids[None] >= shaped[1:]).astype(jnp.int32), axis=0)
    levels = jnp.arange(counts.shape[0], dtype=jnp.int32).reshape(shaped.shape)
    starts = jnp.sum(jnp.where(partition[None] == levels, shaped, 0), axis=0)
    columns = partition * capacity + pool_ids - starts
    return (columns, (slot_lists >= 0).astype(jnp.float32))


def accumulate(getter, present):
    sides = []
    for layer_side in range(2):
        summed = None
        for quad_slot in range(4):
            row_values = getter(quad_slot, layer_side) * present[quad_slot]
            contribution = jnp.einsum(
                "bfxy,bo->ofxy", row_values, offset_table(quad_slot, layer_side), precision=highest
            )
            summed = contribution if summed is None else summed + contribution
        sides.append(summed)
    return (sides[0], sides[1])


def apply_operator(block, stencil, diagonal):
    extended = extended_2(block, (("slab", 2),), 1)
    edge_shape = extended.shape[:4]
    first_column = extended[..., 0].reshape(-1)
    last_column = extended[..., -1].reshape(-1)
    from_left = from_behind(last_column, "dom", 1).reshape(edge_shape + (1,))
    from_right = from_behind(first_column, "dom", -1).reshape(edge_shape + (1,))
    extended = jnp.concatenate([from_left, extended, from_right], axis=4)
    padded = jnp.pad(extended, ((0, 0), (0, 0), (0, 0), (1, 1), (0, 0)))
    floors, across, beside_all = (block.shape[2], block.shape[3], block.shape[4])
    result = diagonal[:, None] * block
    for offset in range(27):
        step_x = offset % 3
        step_y = offset // 3 % 3
        step_z = offset // 9
        result = (
            result
            + stencil[offset]
            * padded[
                :,
                :,
                step_z : step_z + floors,
                step_x : step_x + across,
                step_y : step_y + beside_all,
            ]
        )
    return result


def local_inner(first_block, second_block):
    return jnp.einsum("cvfxy,cwfxy->vw", first_block, second_block, precision=highest)


def mix(block, matrix):
    return jnp.einsum("cvfxy,vw->cwfxy", block, matrix, precision=highest)


def normalize(block, gram_matrix):
    factor = jnp.linalg.cholesky(gram_matrix)
    identity = jnp.eye(gram_matrix.shape[0], dtype=jnp.float32)
    inverse = lax.linalg.triangular_solve(factor, identity, left_side=True, lower=True)
    return (jnp.einsum("cvfxy,wv->cwfxy", block, inverse, precision=highest), factor.T)


def advance(basis_block, image_block, dof_count):
    projection = lax.psum(local_inner(basis_block, image_block), ("slab", "dom")) / dof_count
    residual = image_block - mix(basis_block, projection)
    gram_matrix = lax.psum(local_inner(residual, residual), ("slab", "dom")) / dof_count
    following, upper_factor = normalize(residual, gram_matrix)
    return (following, projection, upper_factor)


def per_device(
    elem_grad,
    elem_stress,
    elem_grade,
    grade_scale,
    part_counts,
    node_lists,
    stiff_diag,
    start_block,
):
    capacity = elem_grad.shape[2]
    counts = part_counts[0]
    columns, present = pool_columns(node_lists, counts, capacity)
    flat_columns = columns.reshape(-1)
    slot_shape = node_lists.shape
    scales = grade_lookup(elem_grade, grade_scale)
    matrices = element_matrices(elem_grad, elem_stress, scales).reshape(64, capacity)
    shard_piece = lax.all_gather(matrices, "dom", axis=1, tiled=True)
    inside = (flat_columns >= 0) & (flat_columns < shard_piece.shape[1])
    selected = jnp.take(shard_piece, jnp.clip(flat_columns, 0, shard_piece.shape[1] - 1), axis=1)
    picked = jnp.where(inside[None, :], selected, 0.0)
    picked = picked.reshape((8, 8) + slot_shape)

    def getter(quad_slot, layer_side):
        return picked[quad_slot + 4 * layer_side, :, quad_slot]

    bottom, top_side = accumulate(getter, present)
    below = passed_along(bottom[:, 0], "slab", -1)
    stencil = top_side + jnp.concatenate([bottom[:, 1:], below[:, None]], axis=1)
    dof_count = (
        3
        * start_block.shape[2]
        * start_block.shape[3]
        * start_block.shape[4]
        * lax.axis_size("slab")
        * lax.axis_size("dom")
    )
    start_gram = lax.psum(local_inner(start_block, start_block), ("slab", "dom")) / dof_count
    first, start_factor = normalize(start_block, start_gram)
    image_block = apply_operator(first, stencil, stiff_diag)
    second, alpha_one, beta_one = advance(first, image_block, dof_count)
    image_block = apply_operator(second, stencil, stiff_diag) - mix(first, beta_one.T)
    third, alpha_two, beta_two = advance(second, image_block, dof_count)
    return (third, jnp.stack([alpha_one, alpha_two]), jnp.stack([start_factor, beta_one, beta_two]))


def solution(mesh):
    in_specs = (
        P(None, None, ("slab", "dom")),
        P(None, ("slab", "dom")),
        P(("slab", "dom")),
        P(),
        P("slab", None),
        P(None, "slab", None, "dom"),
        P(None, "slab", None, "dom"),
        P(None, None, "slab", None, "dom"),
    )
    out_specs = (P(None, None, "slab", None, "dom"), P(), P())
    return jax.shard_map(
        per_device, mesh=mesh, in_specs=in_specs, out_specs=out_specs, check_vma=False
    )
```

profile of v0, /device:TPU:1, one launch (start us, length us, event | category | flops | bytes accessed | tf_op | source)
XLA Modules:
  0.0 704.9 jit_solution(14707492040384633531)
XLA Ops:
  9.1 7.5 %copy.136 = f32[3,3,5376]{1,0,2:T(4,128)} copy(f32[3,3,5376]{2,1,0:T(4,128)S(1)} %pad_maximum_fusion.18) | data formatting | bytes 387072 | tf_op jit(solution)/shard_map/stack | solution.py:55
  16.6 7.2 %copy.137 = f32[3,8,5376]{1,0,2:T(4,128)} copy(f32[3,8,5376]{2,1,0:T(8,128)S(1)} %copy-done.12) | data formatting | bytes 1032192 | tf_op args[0]
  23.9 39.3 %fusion.144 = f32[5376,3,8]{2,1,0:T(4,128)S(1)} fusion(f32[3,3,5376]{1,0,2:T(4,128)} %copy.136, f32[3,8,5376]{1,0,2:T(4,128)} %copy.137), kind=kOutput, calls=%fused_computation.282 | convolution fusion | flops 4644864 | bytes 1225728 | tf_op jit(solution)/shard_map/ik...,kb...->ib.../dot_general | solution.py:71
  63.5 57.4 %multiply_bitcast_fusion = f32[8,8,5376]{0,1,2:T(8,128)} fusion(f32[5376]{0:T(1024)S(1)} %convolution_reduce_fusion, f32[3,8,5376]{1,0,2:T(4,128)S(1)} %copy-done.2, f32[5376,3,8]{2,1,0:T(4,128)S(1)} %fusion.144), kind=kOutput, calls=%fused_computation.1 | convolution fusion | flops 12730368 | bytes 2429952 | tf_op jit(solution)/shard_map/ia...,ib...->ab.../dot_general | solution.py:72
  120.9 12.2 %copy.139 = f32[8,8,5376]{2,1,0:T(8,128)S(1)} copy(f32[8,8,5376]{0,1,2:T(8,128)} %multiply_bitcast_fusion) | data formatting | bytes 2752512 | tf_op jit(solution)/shard_map/mul | solution.py:72
  136.2 82.3 %psum.35 = f32[32,32]{0,1:T(8,128)S(1)} all-reduce(f32[32,32]{0,1:T(8,128)S(1)} %convolution_bitcast_fusion.10), channel_id=1, replica_groups=mesh['slab'=64,'dom'=4] {'slab','dom'}, use_global_device_ids=true, to_apply=%region_0.0 | all-reduce | flops 1024 | bytes 8192 | tf_op jit(solution)/shard_map/psum | solution.py:189
  218.5 2.9 cholesky.59
  233.9 4.8 collective-permute-done.2
  240.6 3.8 copy.154
  247.5 2.5 collective-permute-start.4
  253.4 3.5 copy.157
  256.9 4.5 select_maximum_fusion.4
  261.4 31.8 %gather_fusion = f32[8192,64]{1,0:T(8,128)} fusion(f32[64,21504]{0,1:T(8,128)} %all-gather.2.cloned.1.call-done, s32[8192]{0:T(1024)S(1)} %copy-done.13), kind=kCustom, calls=%fused_computation | custom fusion | bytes 4227072 | tf_op jit(solution)/shard_map/jit(_take)/gather | solution.py:171
  293.2 3.8 copy.141
  304.9 2.7 collective-permute-done
  308.5 5.3 fusion.41
  314.9 81.3 %psum.36 = f32[32,32]{0,1:T(8,128)S(1)} all-reduce(f32[32,32]{0,1:T(8,128)S(1)} %convolution_bitcast_fusion.9), channel_id=1, replica_groups=mesh['slab'=64,'dom'=4] {'slab','dom'}, use_global_device_ids=true, to_apply=%region_6.9 | all-reduce | flops 1024 | bytes 8192 | tf_op jit(solution)/shard_map/psum | solution.py:145
  397.7 73.5 %psum.37 = f32[32,32]{0,1:T(8,128)S(1)} all-reduce(f32[32,32]{0,1:T(8,128)S(1)} %convolution_bitcast_fusion.8), channel_id=1, replica_groups=mesh['slab'=64,'dom'=4] {'slab','dom'}, use_global_device_ids=true, to_apply=%region_7.10 | all-reduce | flops 1024 | bytes 8192 | tf_op jit(solution)/shard_map/psum | solution.py:147
  471.3 2.9 cholesky.70
  479.8 3.5 collective-permute-start.5
  485.2 2.8 collective-permute-done.5
  488.0 4.4 collective-permute-done.6
  495.0 4.4 copy.163
  501.3 3.0 copy.164
  506.0 2.7 collective-permute-start.8
  510.9 3.2 copy.165
  515.8 4.4 copy.166
  520.4 3.4 select_maximum_fusion
  524.1 7.2 %fusion.10 = f32[3,32,2,8,128]{4,1,3,2,0:T(8,128)S(1)} fusion(f32[3,32,4,10,130]{4,1,3,2,0:T(8,128)S(1)} %select_maximum_fusion, f32[3,32,4,8,1]{4,1,3,2,0:T(8,128)S(1)} %copy-done.5, f32[3,32,1,8,128]{4,1,3,2,0:T(8,128)S(1)} %copy-done.11, f32[3,32,2,8,128]{4,1,3,2,0:T(8,128)S(1)} %convolution_bitcast_fusion.3, ...), kind=kOutput, calls=%fused_computation.45 | convolution fusion | flops 90442752 | bytes 17575936 | tf_op jit(solution)/shard_map/cvfxy,vw->cwfxy/dot_general | solution.py:134
  533.0 78.2 %psum.38 = f32[32,32]{0,1:T(8,128)S(1)} all-reduce(f32[32,32]{0,1:T(8,128)S(1)} %convolution_bitcast_fusion.7), channel_id=1, replica_groups=mesh['slab'=64,'dom'=4] {'slab','dom'}, use_global_device_ids=true, to_apply=%region_8.11 | all-reduce | flops 1024 | bytes 8192 | tf_op jit(solution)/shard_map/psum | solution.py:145
  613.9 73.4 %psum.39 = f32[32,32]{0,1:T(8,128)S(1)} all-reduce(f32[32,32]{0,1:T(8,128)S(1)} %convolution_bitcast_fusion.6), channel_id=1, replica_groups=mesh['slab'=64,'dom'=4] {'slab','dom'}, use_global_device_ids=true, to_apply=%region_9.12 | all-reduce | flops 1024 | bytes 8192 | tf_op jit(solution)/shard_map/psum | solution.py:147
  687.4 2.9 cholesky.81
  (284 shorter events, 66.5 us)
Async XLA Ops:
  7.2 56.1 %copy-start = (f32[16]{0:T(128)S(1)}, f32[16]{0:T(128)}, u32[]{:S(2)}) copy-start(f32[16]{0:T(128)} %param.22) | copy-start | bytes 196
  7.2 254.2 %all-gather.2.cloned.1.call-start = ((), (), s32[]{:S(2)}) async-start(), calls=%async_computation | async-start | bytes 13762560 | tf_op jit(solution)/shard_map/all_gather | solution.py:169
  9.1 7.5 %copy-start.12 = (f32[3,8,5376]{2,1,0:T(8,128)S(1)}, f32[3,8,5376]{2,1,0:T(8,128)}, u32[]{:S(2)}) copy-start(f32[3,8,5376]{2,1,0:T(8,128)} %param.19) | copy-start | bytes 1548292
  23.9 39.4 %copy-start.89 = (s32[5376]{0:T(1024)S(1)}, s32[5376]{0:T(1024)}, u32[]{:S(2)}) copy-start(s32[5376]{0:T(1024)} %param.21) | copy-start | bytes 64516
  23.9 39.6 %copy-start.2 = (f32[3,8,5376]{1,0,2:T(4,128)S(1)}, f32[3,8,5376]{1,0,2:T(4,128)}, u32[]{:S(2)}) copy-start(f32[3,8,5376]{1,0,2:T(4,128)} %copy.137) | copy-start | bytes 1548292
  135.2 96.4 %copy-start.90 = (s32[1,4]{1,0:T(1,128)S(1)}, s32[1,4]{1,0:T(1,128)}, u32[]{:S(2)}) copy-start(s32[1,4]{1,0:T(1,128)} %param.23) | copy-start | bytes 52
  135.2 96.7 %copy-start.14 = (s32[4,2,8,128]{3,2,1,0:T(8,128)S(1)}, s32[4,2,8,128]{3,2,1,0:T(8,128)}, u32[]{:S(2)}) copy-start(s32[4,2,8,128]{3,2,1,0:T(8,128)} %param.24) | copy-start | bytes 98308
  227.1 6.9 collective-permute-start.1
  229.2 9.5 %collective-permute-start.2 = (f32[3,32,1,8,128]{4,1,3,2,0:T(8,128)S(1)}, f32[3,32,1,8,128]{4,1,3,2,0:T(8,128)S(1)}, u32[]{:S(2)}, u32[]{:S(2)}) collective-permute-start(f32[3,32,1,8,128]{4,1,3,2,0:T(8,128)S(1)} %get-tuple-element.40), channel_id=1, source_target_pairs={{4,0},{8,4},{12,8},{16,12},{20,16},{24,20},{28,24},{32,28},{36,32}... | collective-permute-start | bytes 1179656 | tf_op jit(solution)/shard_map/ppermute | solution.py:20
  238.7 18.1 %copy-start.6 = (f32[3,32,1,8,128]{4,1,3,2,0:T(8,128)}, f32[3,32,1,8,128]{4,1,3,2,0:T(8,128)S(1)}, u32[]{:S(2)}) copy-start(f32[3,32,1,8,128]{4,1,3,2,0:T(8,128)S(1)} %collective-permute-done.2) | copy-start | bytes 1179652
  238.8 11.1 %copy-start.15 = (f32[4,2,8,128]{3,2,1,0:T(8,128)S(1)}, f32[4,2,8,128]{3,2,1,0:T(8,128)}, u32[]{:S(2)}) copy-start(f32[4,2,8,128]{3,2,1,0:T(8,128)} %get-tuple-element.80) | copy-start | bytes 98308
  244.5 6.0 collective-permute-start.3
  247.5 5.7 collective-permute-start.4
  293.2 5.9 copy-start.78
  299.2 8.4 %copy-start.81 = (f32[8,27,1,1]{1,0,3,2:T(8,128)S(1)}, f32[8,27,1,1]{1,0,3,2:T(8,128)}, u32[]{:S(2)}) copy-start(f32[8,27,1,1]{1,0,3,2:T(8,128)} %constant.100) | copy-start | bytes 2596
  299.4 9.0 %copy-start.3 = (f32[3,32,4,10,130]{4,1,3,2,0:T(8,128)S(1)}, f32[3,32,4,10,130]{4,1,3,2,0:T(8,128)}, u32[]{:S(2)}) copy-start(f32[3,32,4,10,130]{4,1,3,2,0:T(8,128)} %select_maximum_fusion.4) | copy-start | bytes 5990404
  299.4 9.0 %copy-start.4 = (f32[3,32,4,8,1]{4,1,3,2,0:T(8,128)S(1)}, f32[3,32,4,8,1]{4,1,3,2,0:T(8,128)}, u32[]{:S(2)}) copy-start(f32[3,32,4,8,1]{4,1,3,2,0:T(8,128)} %copy.157) | copy-start | bytes 36868
  299.5 9.0 %copy-start.7 = (f32[3,32,1,8,128]{4,1,3,2,0:T(8,128)S(1)}, f32[3,32,1,8,128]{4,1,3,2,0:T(8,128)}, u32[]{:S(2)}) copy-start(f32[3,32,1,8,128]{4,1,3,2,0:T(8,128)} %copy-done.6) | copy-start | bytes 1179652
  299.5 9.0 %copy-start.79 = (f32[3,2,8,128]{3,2,1,0:T(8,128)S(1)}, f32[3,2,8,128]{3,2,1,0:T(8,128)}, u32[]{:S(2)}) copy-start(f32[3,2,8,128]{3,2,1,0:T(8,128)} %param.25) | copy-start | bytes 73732
  301.3 6.3 collective-permute-start
  308.1 5.7 copy-start.21
  308.1 5.7 copy-start.23
  308.1 5.7 copy-start.25
  308.1 5.7 copy-start.27
  479.8 8.2 %collective-permute-start.5 = (f32[3,32,1,8,128]{4,1,3,2,0:T(8,128)S(1)}, f32[3,32,1,8,128]{4,1,3,2,0:T(8,128)S(1)}, u32[]{:S(2)}, u32[]{:S(2)}) collective-permute-start(f32[3,32,1,8,128]{4,1,3,2,0:T(8,128)S(1)} %get-tuple-element.37), channel_id=1, source_target_pairs={{0,4},{4,8},{8,12},{12,16},{16,20},{20,24},{24,28},{28,32},{32,36}... | collective-permute-start | bytes 1179656 | tf_op jit(solution)/shard_map/ppermute | solution.py:18
  483.3 9.1 %collective-permute-start.6 = (f32[3,32,1,8,128]{4,1,3,2,0:T(8,128)S(1)}, f32[3,32,1,8,128]{4,1,3,2,0:T(8,128)S(1)}, u32[]{:S(2)}, u32[]{:S(2)}) collective-permute-start(f32[3,32,1,8,128]{4,1,3,2,0:T(8,128)S(1)} %get-tuple-element.38), channel_id=1, source_target_pairs={{4,0},{8,4},{12,8},{16,12},{20,16},{24,20},{28,24},{32,28},{36,32}... | collective-permute-start | bytes 1179656 | tf_op jit(solution)/shard_map/ppermute | solution.py:20
  501.1 8.2 %collective-permute-start.7 = (f32[3072]{0:T(1024)}, f32[3072]{0:T(1024)}, u32[]{:S(2)}, u32[]{:S(2)}) collective-permute-start(f32[3072]{0:T(1024)} %reshape_squeeze.14), channel_id=1, source_target_pairs={{0,1},{1,2},{2,3},{3,0},{4,5},{5,6},{6,7},{7,4},{8,9},{9,10},{10,1... | collective-permute-start | bytes 36872 | tf_op jit(solution)/shard_map/ppermute | solution.py:30
  506.0 8.1 %collective-permute-start.8 = (f32[3072]{0:T(1024)}, f32[3072]{0:T(1024)}, u32[]{:S(2)}, u32[]{:S(2)}) collective-permute-start(f32[3072]{0:T(1024)} %reshape_squeeze.15), channel_id=1, source_target_pairs={{0,3},{1,0},{2,1},{3,2},{4,7},{5,4},{6,5},{7,6},{8,11},{9,8},{10,9... | collective-permute-start | bytes 36872 | tf_op jit(solution)/shard_map/ppermute | solution.py:30
  532.2 159.4 %copy-start.18 = (f32[1,32,32]{1,2,0:T(8,128)S(1)}, f32[1,32,32]{1,2,0:T(8,128)}, u32[]{:S(2)}) copy-start(f32[1,32,32]{1,2,0:T(8,128)} %get-tuple-element.84) | copy-start | bytes 12292
  532.2 159.4 %copy-start.19 = (f32[1,32,32]{1,2,0:T(8,128)S(1)}, f32[1,32,32]{1,2,0:T(8,128)}, u32[]{:S(2)}) copy-start(f32[1,32,32]{1,2,0:T(8,128)} %get-tuple-element.86) | copy-start | bytes 12292
  532.2 160.2 %copy-start.20 = (f32[1,32,32]{1,2,0:T(8,128)S(1)}, f32[1,32,32]{1,2,0:T(8,128)}, u32[]{:S(2)}) copy-start(f32[1,32,32]{1,2,0:T(8,128)} %multiply_bitcast_fusion.2) | copy-start | bytes 12292
  532.2 165.7 %copy-start.1 = (f32[16]{0:T(128)S(1)}, f32[16]{0:T(128)}, u32[]{:S(2)}) copy-start(f32[16]{0:T(128)} %param.22) | copy-start | bytes 196
  (69 other events, 288.6 us)
Sparse Core Ops, SparseCore 0:
  135.3 112.6 all-gather.1
where the time goes:
time: 713 us; the launch traced here: 705 us
  blocking collectives  389 us (55%)
  matrix products  117 us (16%)
  local copies, waits for them, and re-layouts  112 us (16%)
  other arithmetic  37.7 us (5%)
  starting transfers between devices  18 us (3%)
  between operations  15.9 us (2%)
  waiting for transfers between devices  15.2 us (2%)
    psum x2, blocking collectives, advance(): lax.psum(local_inner(basis_block, image_block), ('slab', 'dom')) / dof_count  160 us
    psum x2, blocking collectives, advance(): lax.psum(local_inner(residual, residual), ('slab', 'dom')) / dof_count  147 us
    psum x1, blocking collectives, per_device(): lax.psum(local_inner(start_block, start_block), ('slab', 'dom')) / dof_count  82.3 us
    dot_general x1, matrix products, element_matrices(): jnp.einsum('ia...,ib...->ab...', gradients, pushed, precision=highest)  57.4 us
    dot_general x1, matrix products, element_matrices(): jnp.einsum('ik...,kb...->ib...', stress_matrix(stress), gradients, precis...  39.3 us
    gather x2, local copies, waits for them, and re-layouts, per_device(): jnp.take(shard_piece, jnp.clip(flat_columns, 0, shard_piece.shape[1] - 1)...  35.7 us
  transfers between devices with their start and end apart: 10, of which 5 were waited for; matrix products, arithmetic and copies ran while one was open for 6% of the time, Pallas kernels for 0%

commit v1 on v0

--- a/solution.py
+++ b/solution.py
@@ -5,6 +5,11 @@
 from jax.sharding import PartitionSpec as P
 
 highest = lax.Precision.HIGHEST
+
+
+def view_field(values):
+    step_out = lax.all_gather(values, axis_name=("slab", "dom"))
+    return jnp.sum(step_out, 0)
 
 
 def extended_2(cells, sides, width):
@@ -142,7 +147,7 @@
 
 
 def advance(basis_block, image_block, dof_count):
-    projection = lax.psum(local_inner(basis_block, image_block), ("slab", "dom")) / dof_count
+    projection = view_field(local_inner(basis_block, image_block)) / dof_count
     residual = image_block - mix(basis_block, projection)
     gram_matrix = lax.psum(local_inner(residual, residual), ("slab", "dom")) / dof_count
     following, upper_factor = normalize(residual, gram_matrix)

time: 713 us -> 793 us (1.11)
  waiting for transfers between devices: 15.2 us -> 248 us
  blocking collectives: 389 us -> 232 us
    all_gather x0 -> x2, waiting for transfers between devices: none -> 232 us  [view_field(): step_out = lax.all_gather(values, axis_name=('slab', 'dom'))]
    psum x2 -> x0, blocking collectives: 160 us -> none  [advance(): lax.psum(local_inner(basis_block, image_block), ('slab', 'dom')) / dof_count]
  transfers between devices with their start and end apart: 10 -> 12, of which waited for: 5 -> 7; matrix products, arithmetic and copies ran while one was open for 6% -> 5% of each run, Pallas kernels for 0% -> 0%
where the time goes in v1:
time: 793 us; the launch traced here: 786 us
  waiting for transfers between devices  248 us (31%)
  blocking collectives  232 us (29%)
  matrix products  118 us (15%)
  local copies, waits for them, and re-layouts  113 us (14%)
  other arithmetic  42.8 us (5%)
  starting transfers between devices  17.3 us (2%)
  between operations  15.6 us (2%)
    all_gather x2, waiting for transfers between devices, view_field(): step_out = lax.all_gather(values, axis_name=('slab', 'dom'))  232 us
    psum x2, blocking collectives, advance(): lax.psum(local_inner(residual, residual), ('slab', 'dom')) / dof_count  150 us
    psum x1, blocking collectives, per_device(): lax.psum(local_inner(start_block, start_block), ('slab', 'dom')) / dof_count  82.3 us
    dot_general x1, matrix products, element_matrices(): jnp.einsum('ia...,ib...->ab...', gradients, pushed, precision=highest)  57.6 us
    dot_general x1, matrix products, element_matrices(): jnp.einsum('ik...,kb...->ib...', stress_matrix(stress), gradients, precis...  39.3 us
    gather x2, local copies, waits for them, and re-layouts, per_device(): jnp.take(shard_piece, jnp.clip(flat_columns, 0, shard_piece.shape[1] - 1)...  35.6 us
  transfers between devices with their start and end apart: 12, of which 7 were waited for; matrix products, arithmetic and copies ran while one was open for 5% of the time, Pallas kernels for 0%

profile of v1, /device:TPU:1, one launch (start us, length us, event | category | flops | bytes accessed | tf_op | source)
XLA Modules:
  0.0 785.6 jit_solution(7153947441334769789)
XLA Ops:
  9.1 7.5 copy.177
  16.7 7.2 copy.178
  23.9 39.3 %fusion.144 = f32[5376,3,8]{2,1,0:T(4,128)S(1)} fusion(f32[3,3,5376]{1,0,2:T(4,128)} %copy.177, f32[3,8,5376]{1,0,2:T(4,128)} %copy.178), kind=kOutput, calls=%fused_computation.282 | convolution fusion | flops 4644864 | bytes 1225728 | tf_op jit(solution)/shard_map/ik...,kb...->ib.../dot_general | solution.py:76
  63.5 57.6 %multiply_bitcast_fusion = f32[8,8,5376]{0,1,2:T(8,128)} fusion(f32[5376]{0:T(1024)S(1)} %convolution_reduce_fusion, f32[3,8,5376]{1,0,2:T(4,128)S(1)} %copy-done.2, f32[5376,3,8]{2,1,0:T(4,128)S(1)} %fusion.144), kind=kOutput, calls=%fused_computation.1 | convolution fusion | flops 12730368 | bytes 2429952 | tf_op jit(solution)/shard_map/ia...,ib...->ab.../dot_general | solution.py:77
  121.1 12.2 %copy.180 = f32[8,8,5376]{2,1,0:T(8,128)S(1)} copy(f32[8,8,5376]{0,1,2:T(8,128)} %multiply_bitcast_fusion) | data formatting | bytes 2752512 | tf_op jit(solution)/shard_map/mul | solution.py:77
  136.5 82.3 %psum.21 = f32[32,32]{0,1:T(8,128)S(1)} all-reduce(f32[32,32]{0,1:T(8,128)S(1)} %convolution_bitcast_fusion.10), channel_id=1, replica_groups=mesh['slab'=64,'dom'=4] {'slab','dom'}, use_global_device_ids=true, to_apply=%region_0.0 | all-reduce | flops 1024 | bytes 8192 | tf_op jit(solution)/shard_map/psum | solution.py:194
  218.9 2.9 cholesky.59
  234.3 4.8 collective-permute-done.2
  240.9 3.8 copy.195
  253.8 3.5 copy.198
  257.2 4.5 select_maximum_fusion.4
  261.8 31.8 %gather_fusion = f32[8192,64]{1,0:T(8,128)} fusion(f32[64,21504]{0,1:T(8,128)} %all-gather.6.cloned.1.call-done, s32[8192]{0:T(1024)S(1)} %copy-done.15), kind=kCustom, calls=%fused_computation | custom fusion | bytes 4227072 | tf_op jit(solution)/shard_map/jit(_take)/gather | solution.py:176
  293.6 3.8 copy.182
  305.3 2.7 collective-permute-done
  308.8 5.4 fusion.41
  315.9 117.9 %all-gather.8.cloned.1.call-done = f32[8192,32]{1,0:T(8,128)} async-done(((f32[32,32]{1,0:T(8,128)}), f32[8192,32]{1,0:T(8,128)}) %all-gather.8.cloned.1.call-update) | async-done | bytes 1048592 | tf_op jit(solution)/shard_map/all_gather | solution.py:11
  438.0 74.9 %psum.22 = f32[32,32]{0,1:T(8,128)S(1)} all-reduce(f32[32,32]{0,1:T(8,128)S(1)} %convolution_bitcast_fusion.8), channel_id=1, replica_groups=mesh['slab'=64,'dom'=4] {'slab','dom'}, use_global_device_ids=true, to_apply=%region_7.10 | all-reduce | flops 1024 | bytes 8192 | tf_op jit(solution)/shard_map/psum | solution.py:152
  512.9 2.9 cholesky.70
  521.3 2.7 collective-permute-start.5
  525.9 2.8 collective-permute-done.5
  528.7 4.4 collective-permute-done.6
  535.7 4.4 copy.204
  542.0 3.1 copy.205
  546.8 2.7 collective-permute-start.8
  551.1 3.2 copy.206
  556.0 4.4 copy.207
  560.6 3.4 select_maximum_fusion
  564.3 7.2 fusion.10
  574.5 114.4 %all-gather.10.cloned.1.call-done = f32[8192,32]{1,0:T(8,128)} async-done(((f32[32,32]{1,0:T(8,128)}), f32[8192,32]{1,0:T(8,128)}) %all-gather.10.cloned.1.call-update) | async-done | bytes 1048592 | tf_op jit(solution)/shard_map/all_gather | solution.py:11
  689.0 2.6 reduce_sum.39
  693.2 75.1 %psum.23 = f32[32,32]{0,1:T(8,128)S(1)} all-reduce(f32[32,32]{0,1:T(8,128)S(1)} %convolution_bitcast_fusion.6), channel_id=1, replica_groups=mesh['slab'=64,'dom'=4] {'slab','dom'}, use_global_device_ids=true, to_apply=%region_9.12 | all-reduce | flops 1024 | bytes 8192 | tf_op jit(solution)/shard_map/psum | solution.py:152
  768.4 2.9 cholesky.81
  (292 shorter events, 71.9 us)
Async XLA Ops:
  7.2 56.1 %copy-start = (f32[16]{0:T(128)S(1)}, f32[16]{0:T(128)}, u32[]{:S(2)}) copy-start(f32[16]{0:T(128)} %param.22) | copy-start | bytes 196
  7.2 254.6 %all-gather.6.cloned.1.call-start = ((), (), s32[]{:S(2)}) async-start(), calls=%async_computation | async-start | bytes 13762560 | tf_op jit(solution)/shard_map/all_gather | solution.py:174
  9.1 7.5 copy-start.13
  23.9 39.3 %copy-start.89 = (s32[5376]{0:T(1024)S(1)}, s32[5376]{0:T(1024)}, u32[]{:S(2)}) copy-start(s32[5376]{0:T(1024)} %param.21) | copy-start | bytes 64516
  23.9 39.6 %copy-start.2 = (f32[3,8,5376]{1,0,2:T(4,128)S(1)}, f32[3,8,5376]{1,0,2:T(4,128)}, u32[]{:S(2)}) copy-start(f32[3,8,5376]{1,0,2:T(4,128)} %copy.178) | copy-start | bytes 1548292
  135.5 96.5 %copy-start.90 = (s32[1,4]{1,0:T(1,128)S(1)}, s32[1,4]{1,0:T(1,128)}, u32[]{:S(2)}) copy-start(s32[1,4]{1,0:T(1,128)} %param.23) | copy-start | bytes 52
  135.5 96.8 %copy-start.16 = (s32[4,2,8,128]{3,2,1,0:T(8,128)S(1)}, s32[4,2,8,128]{3,2,1,0:T(8,128)}, u32[]{:S(2)}) copy-start(s32[4,2,8,128]{3,2,1,0:T(8,128)} %param.24) | copy-start | bytes 98308
  135.5 298.3 %all-gather.8.cloned.1.call-start = ((), (), s32[]{:S(2)}) async-start(), calls=%async_computation.1 | async-start | bytes 4210688 | tf_op jit(solution)/shard_map/all_gather | solution.py:11
  227.4 6.8 collective-permute-start.1
  229.6 9.5 %collective-permute-start.2 = (f32[3,32,1,8,128]{4,1,3,2,0:T(8,128)S(1)}, f32[3,32,1,8,128]{4,1,3,2,0:T(8,128)S(1)}, u32[]{:S(2)}, u32[]{:S(2)}) collective-permute-start(f32[3,32,1,8,128]{4,1,3,2,0:T(8,128)S(1)} %get-tuple-element.43), channel_id=1, source_target_pairs={{4,0},{8,4},{12,8},{16,12},{20,16},{24,20},{28,24},{32,28},{36,32}... | collective-permute-start | bytes 1179656 | tf_op jit(solution)/shard_map/ppermute | solution.py:25
  239.1 18.2 %copy-start.6 = (f32[3,32,1,8,128]{4,1,3,2,0:T(8,128)}, f32[3,32,1,8,128]{4,1,3,2,0:T(8,128)S(1)}, u32[]{:S(2)}) copy-start(f32[3,32,1,8,128]{4,1,3,2,0:T(8,128)S(1)} %collective-permute-done.2) | copy-start | bytes 1179652
  239.2 11.1 %copy-start.17 = (f32[4,2,8,128]{3,2,1,0:T(8,128)S(1)}, f32[4,2,8,128]{3,2,1,0:T(8,128)}, u32[]{:S(2)}) copy-start(f32[4,2,8,128]{3,2,1,0:T(8,128)} %get-tuple-element.83) | copy-start | bytes 98308
  244.9 6.1 collective-permute-start.3
  247.9 5.6 collective-permute-start.4
  293.6 5.9 copy-start.78
  299.5 8.4 %copy-start.81 = (f32[8,27,1,1]{1,0,3,2:T(8,128)S(1)}, f32[8,27,1,1]{1,0,3,2:T(8,128)}, u32[]{:S(2)}) copy-start(f32[8,27,1,1]{1,0,3,2:T(8,128)} %constant.100) | copy-start | bytes 2596
  299.8 9.0 %copy-start.3 = (f32[3,32,4,10,130]{4,1,3,2,0:T(8,128)S(1)}, f32[3,32,4,10,130]{4,1,3,2,0:T(8,128)}, u32[]{:S(2)}) copy-start(f32[3,32,4,10,130]{4,1,3,2,0:T(8,128)} %select_maximum_fusion.4) | copy-start | bytes 5990404
  299.8 9.0 %copy-start.4 = (f32[3,32,4,8,1]{4,1,3,2,0:T(8,128)S(1)}, f32[3,32,4,8,1]{4,1,3,2,0:T(8,128)}, u32[]{:S(2)}) copy-start(f32[3,32,4,8,1]{4,1,3,2,0:T(8,128)} %copy.198) | copy-start | bytes 36868
  299.8 9.0 %copy-start.7 = (f32[3,32,1,8,128]{4,1,3,2,0:T(8,128)S(1)}, f32[3,32,1,8,128]{4,1,3,2,0:T(8,128)}, u32[]{:S(2)}) copy-start(f32[3,32,1,8,128]{4,1,3,2,0:T(8,128)} %copy-done.6) | copy-start | bytes 1179652
  299.8 9.0 %copy-start.79 = (f32[3,2,8,128]{3,2,1,0:T(8,128)S(1)}, f32[3,2,8,128]{3,2,1,0:T(8,128)}, u32[]{:S(2)}) copy-start(f32[3,2,8,128]{3,2,1,0:T(8,128)} %param.25) | copy-start | bytes 73732
  301.7 6.3 collective-permute-start
  308.5 5.7 copy-start.22
  315.9 373.1 %all-gather.10.cloned.1.call-start = ((), (), s32[]{:S(2)}) async-start(), calls=%async_computation.2 | async-start | bytes 4210688 | tf_op jit(solution)/shard_map/all_gather | solution.py:11
  436.4 83.7 %copy-start.14 = (f32[32,32]{0,1:T(8,128)}, f32[32,32]{0,1:T(8,128)S(1)}, u32[]{:S(2)}) copy-start(f32[32,32]{0,1:T(8,128)S(1)} %copy.201) | copy-start | bytes 12292
  521.3 7.4 collective-permute-start.5
  524.0 9.1 %collective-permute-start.6 = (f32[3,32,1,8,128]{4,1,3,2,0:T(8,128)S(1)}, f32[3,32,1,8,128]{4,1,3,2,0:T(8,128)S(1)}, u32[]{:S(2)}, u32[]{:S(2)}) collective-permute-start(f32[3,32,1,8,128]{4,1,3,2,0:T(8,128)S(1)} %get-tuple-element.41), channel_id=1, source_target_pairs={{4,0},{8,4},{12,8},{16,12},{20,16},{24,20},{28,24},{32,28},{36,32}... | collective-permute-start | bytes 1179656 | tf_op jit(solution)/shard_map/ppermute | solution.py:25
  541.8 7.6 collective-permute-start.7
  546.8 7.5 collective-permute-start.8
  573.7 117.9 %copy-start.10 = (f32[3,32,2,8,128]{4,1,3,2,0:T(8,128)S(1)}, f32[3,32,2,8,128]{4,1,3,2,0:T(8,128)}, u32[]{:S(2)}) copy-start(f32[3,32,2,8,128]{4,1,3,2,0:T(8,128)} %copy-done.9) | copy-start | bytes 2359300
  689.0 83.6 %copy-start.20 = (f32[1,32,32]{1,2,0:T(8,128)S(1)}, f32[1,32,32]{1,2,0:T(8,128)}, u32[]{:S(2)}) copy-start(f32[1,32,32]{1,2,0:T(8,128)} %get-tuple-element.87) | copy-start | bytes 12292
  689.0 83.6 %copy-start.21 = (f32[1,32,32]{1,2,0:T(8,128)S(1)}, f32[1,32,32]{1,2,0:T(8,128)}, u32[]{:S(2)}) copy-start(f32[1,32,32]{1,2,0:T(8,128)} %get-tuple-element.89) | copy-start | bytes 12292
  689.0 89.9 %copy-start.1 = (f32[16]{0:T(128)S(1)}, f32[16]{0:T(128)}, u32[]{:S(2)}) copy-start(f32[16]{0:T(128)} %param.22) | copy-start | bytes 196
  (71 other events, 299.5 us)
Sparse Core Ops, SparseCore 0:
  135.6 112.6 all-gather.5
  316.0 117.7 all-gather.7
  573.9 115.0 all-gather.9
